TPU v7x, 512 devices: a whole 4x4x16 slice. The times are simulated.
512 devices in a mesh: fsdp: 32 (over x, z_hi, core), ctx: 16 (over y, z_lo).
Axes of the slice: x: 4, y: 4, z: 16 (z_hi: 4, z_lo: 4; z = z_hi * 4 + z_lo), core: 2. Of those that a mesh axis runs over, the one named last changes fastest.
Arguments:
- features: bfloat16 [3, 16384, 8192], P(None, 'ctx', 'fsdp'), may hold values from -6 to 6
- short_taps: float32 [3, 3, 8192], P(None, None, 'fsdp'), may hold values from -3.5 to 3.5
- decay_rates: float32 [512, 16], P('fsdp'), may hold values from 1.5258789e-05 to 0.1
- mode_gains: float32 [512, 16], P('fsdp'), may hold values from -2.5 to 2.5
- cotangent: bfloat16 [16384, 8192], P('ctx', 'fsdp'), may hold values from -6 to 6
Outputs:
- mixer_output: bfloat16 [16384, 8192], P('ctx', 'fsdp')
- feature_grads: bfloat16 [3, 16384, 8192], P(None, 'ctx', 'fsdp')
- gain_grads: float32 [512, 16], P('fsdp')
- rate_grads: float32 [512, 16], P('fsdp')
All inputs are finite; a program needn't handle non-finite values.
Results may differ from a plain program's by a relative error of at most 0.0048.
Values may be sent and summed in bfloat16 or wider, within the bound.
A program may use at most 64 MiB of HBM per device.

v0:
```python
import jax
import jax.numpy as jnp
from jax import lax
from jax.sharding import PartitionSpec as P

precise = lax.Precision.HIGHEST
threepass = lax.Precision.HIGH


def passed_along(value, axis, steps):
    count = lax.axis_size(axis)
    leading, last = (max(0, -steps), min(count, count - steps))
    return lax.ppermute(value, axis, [(source, source + steps) for source in range(leading, last)])


def diagonal_sums(gram_acc):
    group_count, block_len, width_same = gram_acc.shape
    flipped = jnp.flip(gram_acc, axis=2)
    padded = jnp.concatenate([flipped, jnp.zeros_like(flipped)], axis=2)
    flattened = padded.reshape(group_count, 2 * block_len * block_len)[
        :, : block_len * (2 * block_len - 1)
    ]
    sheared = flattened.reshape(group_count, block_len, 2 * block_len - 1)
    return jnp.sum(sheared, axis=1)[:, block_len - 1 :]


def short_conv(taps_table, row_data, tokens, rim_rows, forward):
    summed = jnp.zeros((3, tokens, row_data.shape[2]), jnp.float32)
    for offset in range(taps_table.shape[1]):
        start_row = rim_rows - offset if forward else offset
        summed = (
            summed + taps_table[:, offset, None, :] * row_data[:, start_row : start_row + tokens, :]
        )
    return summed


def per_device(features, short_taps, decay_rates, mode_gains, cotangent):
    tokens = features.shape[1]
    channels = features.shape[2]
    group_count = decay_rates.shape[0]
    order_count = decay_rates.shape[1]
    members = channels // group_count
    rim_rows = short_taps.shape[1] - 1
    block_len = 128
    block_count = tokens // block_len
    ctx_count = lax.axis_size("ctx")
    ctx_index = lax.axis_index("ctx")
    earlier_rows = passed_along(features[:, tokens - rim_rows :, :], "ctx", 1)
    extended = jnp.concatenate([earlier_rows, features], axis=1)
    shaped = short_conv(short_taps, extended, tokens, rim_rows, True)
    query_part, key_part, value_part = (shaped[0], shaped[1], shaped[2])
    product = (key_part * value_part).astype(jnp.bfloat16)
    adjoint = cotangent * query_part
    grouped_z = product.reshape(tokens, group_count, members)
    grouped_e = adjoint.reshape(tokens, group_count, members)
    mode_coefs = mode_gains * jnp.sqrt(2.0 * decay_rates)
    rate_axis = decay_rates[:, :, None]
    positions = jnp.arange(tokens, dtype=jnp.float32)[None, None, :]
    decay_from = jnp.exp(-rate_axis * positions)
    end_tables = jnp.stack([jnp.flip(decay_from, 2), -jnp.flip(positions * decay_from, 2)])
    end_states = jnp.einsum(
        "kgns,sgm->kngm", end_tables, grouped_z.astype(jnp.float32), precision=threepass
    )
    start_state = jnp.einsum("gnt,tgm->ngm", decay_from, grouped_e, precision=precise)
    local_states = jnp.stack([end_states[0], end_states[1], start_state]).reshape(
        3, order_count, channels
    )
    rate_cols = jnp.repeat(decay_rates.T, members, axis=1)
    everyone = lax.all_gather(local_states[None], "ctx", axis=0, tiled=True)
    device_ids = jnp.arange(ctx_count, dtype=jnp.int32)
    ahead_steps = (ctx_index - 1 - device_ids).astype(jnp.float32)[:, None, None]
    behind_steps = (device_ids - ctx_index - 1).astype(jnp.float32)[:, None, None]
    ahead_weight = jnp.where(
        ahead_steps >= 0, jnp.exp(-rate_cols[None] * (tokens * jnp.maximum(ahead_steps, 0.0))), 0.0
    )
    behind_weight = jnp.where(
        behind_steps >= 0,
        jnp.exp(-rate_cols[None] * (tokens * jnp.maximum(behind_steps, 0.0))),
        0.0,
    )
    prev_state = jnp.sum(ahead_weight * everyone[:, 0], axis=0)
    prev_lagged = jnp.sum(
        ahead_weight * (everyone[:, 1] - tokens * ahead_steps * everyone[:, 0]), axis=0
    )
    next_state = jnp.sum(behind_weight * everyone[:, 2], axis=0)
    lag_axis = jnp.arange(block_len, dtype=jnp.float32)[None, None, :]
    block_pow = jnp.exp(-rate_axis * lag_axis)
    block_after = block_pow * jnp.exp(-rate_axis)
    block_moments = jnp.stack([block_after, (lag_axis + 1.0) * block_after])
    coef_after = mode_coefs[:, :, None] * block_after
    block_ends = jnp.stack([jnp.flip(block_pow, 2), -jnp.flip(lag_axis * block_pow, 2)])
    coef_tail = mode_coefs[:, :, None] * jnp.flip(block_after, 2)
    block_span = jnp.exp(-decay_rates * block_len).T[:, :, None]
    filter_taps = jnp.sum(mode_coefs[:, :, None] * block_pow, axis=1)
    lag_index = (
        jnp.arange(block_len, dtype=jnp.int32)[:, None]
        - jnp.arange(block_len, dtype=jnp.int32)[None, :]
    )
    toeplitz = jnp.where(lag_index[None] >= 0, filter_taps[:, jnp.maximum(lag_index, 0)], 0.0)
    z_blocks = grouped_z.reshape(block_count, block_len, group_count, members)
    e_blocks = grouped_e.reshape(block_count, block_len, group_count, members)

    def forward_block(carried_in, inputs):
        mode_state, lagged, first_acc, lag_acc, gram_acc = carried_in
        z_block, e_block = inputs
        z_wide = z_block.astype(jnp.float32)
        inside_part = jnp.einsum("gts,sgm->tgm", toeplitz, z_wide, precision=threepass)
        carried = jnp.einsum("gnt,ngm->tgm", coef_after, mode_state, precision=precise)
        moments = jnp.einsum("kgnt,tgm->kngm", block_moments, e_block, precision=precise)
        first_acc = first_acc + jnp.sum(moments[0] * mode_state, axis=2)
        lag_acc = lag_acc + jnp.sum(moments[0] * lagged - moments[1] * mode_state, axis=2)
        gram_acc = gram_acc + jnp.einsum("tgm,sgm->gts", e_block, z_wide, precision=precise)
        fresh_part = jnp.einsum("kgns,sgm->kngm", block_ends, z_wide, precision=threepass)
        new_lagged = block_span * lagged - block_len * block_span * mode_state + fresh_part[1]
        new_state = block_span * mode_state + fresh_part[0]
        return ((new_state, new_lagged, first_acc, lag_acc, gram_acc), inside_part + carried)

    zero_state = jnp.zeros((order_count, group_count, members), jnp.float32)
    zero_pairs = jnp.zeros((order_count, group_count), jnp.float32)
    zero_gram = jnp.zeros((group_count, block_len, block_len), jnp.float32)
    final_carry, inner_blocks = lax.scan(
        forward_block,
        (zero_state, zero_state, zero_pairs, zero_pairs, zero_gram),
        (z_blocks, e_blocks),
    )
    first_acc, lag_acc, gram_acc = (final_carry[2], final_carry[3], final_carry[4])

    def backward_block(later_state, e_block):
        inside_part = jnp.einsum("gts,tgm->sgm", toeplitz, e_block, precision=precise)
        carried = jnp.einsum("gns,ngm->sgm", coef_tail, later_state, precision=precise)
        fresh_part = jnp.einsum("gnt,tgm->ngm", block_pow, e_block, precision=precise)
        return (block_span * later_state + fresh_part, inside_part + carried)

    top_state, grad_blocks = lax.scan(backward_block, zero_state, e_blocks, reverse=True)
    prev_grouped = prev_state.reshape(order_count, group_count, members)
    lagged_grouped = prev_lagged.reshape(order_count, group_count, members)
    next_grouped = next_state.reshape(order_count, group_count, members)
    device_after = decay_from * jnp.exp(-rate_axis)
    inner_sum = inner_blocks.reshape(tokens, group_count, members) + jnp.einsum(
        "gnt,ngm->tgm", mode_coefs[:, :, None] * device_after, prev_grouped, precision=precise
    )
    first_moment = jnp.exp(-decay_rates).T[:, :, None] * start_state
    second_moment = jnp.einsum(
        "gnt,tgm->ngm", (positions + 1.0) * device_after, grouped_e, precision=precise
    )
    first_acc = first_acc + jnp.sum(first_moment * prev_grouped, axis=2)
    lag_acc = lag_acc + jnp.sum(
        first_moment * lagged_grouped - second_moment * prev_grouped, axis=2
    )
    device_tail = mode_coefs[:, :, None] * jnp.flip(device_after, 2)
    product_grad = grad_blocks.reshape(tokens, group_count, members) + jnp.einsum(
        "gns,ngm->sgm", device_tail, next_grouped, precision=precise
    )
    lag_totals = diagonal_sums(gram_acc)
    first_total = first_acc.T + jnp.sum(lag_totals[:, None, :] * block_pow, axis=2)
    lag_total = lag_acc.T - jnp.sum(lag_totals[:, None, :] * lag_axis * block_pow, axis=2)
    gain_part = jnp.sqrt(2.0 * decay_rates) * first_total
    rate_part = mode_coefs * (0.5 * first_total + decay_rates * lag_total)
    inner_flat = inner_sum.reshape(tokens, channels)
    mixer_output = (query_part * inner_flat).astype(jnp.bfloat16)
    grad_flat = product_grad.reshape(tokens, channels)
    feature_adj = jnp.stack([cotangent * inner_flat, grad_flat * value_part, grad_flat * key_part])
    later_rows = passed_along(feature_adj[:, :rim_rows, :], "ctx", -1)
    appended = jnp.concatenate([feature_adj, later_rows], axis=1)
    feature_grads = short_conv(short_taps, appended, tokens, rim_rows, False).astype(jnp.bfloat16)
    filter_local = jnp.stack([gain_part, rate_part])
    entry_count = 2 * group_count * order_count * lax.axis_size("fsdp")
    summed = lax.psum(filter_local, "ctx")
    squares = lax.psum(jnp.sum(summed * summed), "fsdp")
    factor = jnp.minimum(1.0, lax.rsqrt(squares / entry_count + 1e-06))
    clipped = summed * factor
    return (mixer_output, feature_grads, clipped[0], clipped[1])


def solution(mesh):
    return jax.shard_map(
        per_device,
        mesh=mesh,
        in_specs=(
            P(None, "ctx", "fsdp"),
            P(None, None, "fsdp"),
            P("fsdp", None),
            P("fsdp", None),
            P("ctx", "fsdp"),
        ),
        out_specs=(P("ctx", "fsdp"), P(None, "ctx", "fsdp"), P("fsdp", None), P("fsdp", None)),
        check_vma=False,
    )
```

profile of v0, /device:TPU:1, one launch (start us, length us, event | category | flops | bytes accessed | tf_op | source)
XLA Modules:
  0.0 575.3 jit_solution(6784911890546579179)
XLA Ops:
  2.2 5.1 collective-permute-start
  14.9 54.5 %gather_fusion = f32[16384,16]{1,0:T(8,128)} fusion(f32[16,128]{0,1:T(8,128)S(1)} %copy.59, s32[16384]{0:T(1024)S(1)} %bitcast_clamp_fusion), kind=kCustom, calls=%fused_computation | custom fusion | bytes 2162688 | tf_op jit(solution)/shard_map/gather | solution.py:99
  69.4 5.2 copy.60
  77.4 2.6 copy.55
  80.0 3.3 rev.26
  87.9 4.8 multiply_add_fusion
  95.4 3.3 fusion.63
  105.0 41.3 %all_gather.3 = f32[16,3,16,256]{3,2,1,0:T(8,128)S(1)} all-gather(f32[1,3,16,256]{3,2,1,0:T(8,128)S(1)} %pad_maximum_fusion.5), channel_id=1, replica_groups=mesh['fsdp'=32,'ctx'=16] {'ctx'}, dimensions={0}, use_global_device_ids=true | all-gather | bytes 835584 | tf_op jit(solution)/shard_map/all_gather | solution.py:69
  154.0 132.3 %while.38 = (s32[]{:T(128)}, f32[16,16,16]{0,2,1:T(8,128)S(1)}, f32[16,16,16]{0,2,1:T(8,128)}, f32[16,16]{0,1:T(8,128)}, f32[16,16]{0,1:T(8,128)}, /*index=5*/f3...) while((s32[]{:T(128)}, f32[16,16,16]{0,2,1:T(8,128)S(1)}, ...), condition=%wide.region_4.5_spmd.clone, body=%wide.region_1.0_spmd.clone.sunk | while | flops 101380864 | bytes 5014714 | solution.py:121
  156.8 2.9 convolution_bitcast_fusion.8
  162.6 4.5 dynamic_update_slice.17
  172.0 2.9 convolution_bitcast_fusion.8
  179.4 4.5 dynamic_update_slice.17
  188.7 2.9 convolution_bitcast_fusion.8
  196.1 4.5 dynamic_update_slice.17
  205.5 2.9 convolution_bitcast_fusion.8
  212.9 4.5 dynamic_update_slice.17
  222.2 2.9 convolution_bitcast_fusion.8
  229.6 4.5 dynamic_update_slice.17
  239.0 2.9 convolution_bitcast_fusion.8
  246.3 4.5 dynamic_update_slice.17
  255.7 2.9 convolution_bitcast_fusion.8
  263.1 4.5 dynamic_update_slice.17
  272.5 2.9 convolution_bitcast_fusion.8
  279.8 4.5 dynamic_update_slice.17
  286.4 5.8 %rev.30 = f32[16,128,128]{2,1,0:T(8,128)} reverse(f32[16,128,128]{2,1,0:T(8,128)S(1)} %get-tuple-element.242), dimensions={2} | reverse | bytes 2097152 | tf_op jit(solution)/shard_map/jit(_flip)/rev | solution.py:18
  296.3 6.3 %reshape.172 = f32[16,128,255]{2,1,0:T(8,128)} reshape(f32[16,32640]{1,0:T(8,128)} %slice.116) | data formatting | bytes 4177920 | tf_op jit(solution)/shard_map/reshape | solution.py:23
  302.6 2.4 reduce_sum.112
  307.9 2.6 fusion.68
  311.3 61.1 %psum.14 = f32[2,16,16]{2,1,0:T(8,128)S(1)} all-reduce(f32[2,16,16]{2,1,0:T(8,128)S(1)} %pad_maximum_fusion.6), channel_id=1, replica_groups=mesh['fsdp'=32,'ctx'=16] {'ctx'}, use_global_device_ids=true, to_apply=%region_15.16 | all-reduce | flops 512 | bytes 4096 | tf_op jit(solution)/shard_map/psum | solution.py:168
  373.0 5.5 rev.29
  378.5 108.7 %psum.15 = f32[]{:T(128)} all-reduce(f32[]{:T(128)} %multiply_reduce_fusion.6), channel_id=1, replica_groups=mesh['fsdp'=32,'ctx'=16] {'fsdp'}, use_global_device_ids=true, to_apply=%region_17.18 | all-reduce | flops 1 | bytes 8 | tf_op jit(solution)/shard_map/psum | solution.py:169
  491.4 49.0 %while.39 = (s32[]{:T(128)}, f32[16,16,16]{0,2,1:T(8,128)S(1)}, f32[8,128,16,16]{1,0,3,2:T(8,128)}, f32[16,16,1]{0,1,2:T(8,128)S(1)}, f32[8,128,16,16]{1,3,2,0:T...) while((s32[]{:T(128)}, f32[16,16,16]{0,2,1:T(8,128)S(1)}, ...), condition=%wide.region_7.8_spmd.clone, body=%wide.region_6.7_spmd.clone.sunk | while | flops 62996484 | bytes 2277520 | solution.py:134
  492.6 4.5 dynamic_update_slice.18
  498.8 4.5 dynamic_update_slice.18
  504.9 4.5 dynamic_update_slice.18
  511.0 4.5 dynamic_update_slice.18
  517.2 4.5 dynamic_update_slice.18
  523.3 4.5 dynamic_update_slice.18
  529.4 4.5 dynamic_update_slice.18
  535.5 4.5 dynamic_update_slice.18
  540.4 2.5 reshape.168
  543.0 2.6 fusion.61
  547.3 2.4 reshape.164
  549.6 2.6 fusion.62
  558.4 9.5 %collective-permute-done.1 = f32[3,2,256]{1,2,0:T(8,128)S(1)} collective-permute-done((f32[3,2,256]{1,2,0:T(8,128)S(1)}, f32[3,2,256]{1,2,0:T(8,128)S(1)}, u32[]{:S(2)}, u32[]{:S(2)}) %collective-permute-start.1) | collective-permute-done | bytes 6176 | tf_op jit(solution)/shard_map/ppermute | solution.py:13
  569.5 3.3 fusion.54
  572.8 2.6 copy.77
  (215 shorter events, 140.8 us)
Async XLA Ops:
  2.2 85.7 %collective-permute-start = (bf16[3,2,256]{1,2,0:T(8,128)(2,1)}, bf16[3,2,256]{1,2,0:T(8,128)(2,1)}, u32[]{:S(2)}, u32[]{:S(2)}) collective-permute-start(bf16[3,2,256]{1,2,0:T(8,128)(2,1)} %copy.56), channel_id=1, source_target_pairs={{0,1},{1,2},{2,3},{3,4},{4,5},{5,6},{6,7},{7,8},{8,9},{9,10},{10,1... | collective-permute-start | bytes 9224 | tf_op jit(solution)/shard_map/ppermute | solution.py:13
  10.3 4.0 copy-start.19
  10.3 4.3 copy-start.17
  10.3 3.4 copy-start.29
  76.7 6.5 %copy-start.28 = (f32[3,1,256]{2,1,0:T(1,128)S(1)}, f32[3,1,256]{2,1,0:T(1,128)}, u32[]{:S(2)}) copy-start(f32[3,1,256]{2,1,0:T(1,128)} %get-tuple-element.483) | copy-start | bytes 9220
  77.4 7.9 %copy-start.27 = (f32[16,16]{0,1:T(8,128)S(1)}, f32[16,16]{0,1:T(8,128)}, u32[]{:S(2)}) copy-start(f32[16,16]{0,1:T(8,128)} %get-tuple-element.489) | copy-start | bytes 3076
  83.2 4.6 copy-start.25
  92.7 1.6 copy-start
  92.7 2.6 copy-start.10
  92.7 2.7 copy-start.11
  102.1 49.1 %copy-start.8 = (f32[1024,256]{0,1:T(8,128)}, f32[1024,256]{0,1:T(8,128)S(1)}, u32[]{:S(2)}) copy-start(f32[1024,256]{0,1:T(8,128)S(1)} %convert_multiply_fusion.1) | copy-start | bytes 3145732
  103.6 47.8 %copy-start.15 = (f32[16,16,16]{2,1,0:T(8,128)}, f32[16,16,16]{2,1,0:T(8,128)S(1)}, u32[]{:S(2)}) copy-start(f32[16,16,16]{2,1,0:T(8,128)S(1)} %fusion.75) | copy-start | bytes 49156
  150.9 1.0 copy-start.12
  296.3 10.9 %copy-start.14 = (f32[16,256]{0,1:T(8,128)S(1)}, f32[16,256]{0,1:T(8,128)}, u32[]{:S(2)}) copy-start(f32[16,256]{0,1:T(8,128)} %copy.70) | copy-start | bytes 49156
  296.3 10.9 %copy-start.16 = (f32[16,16,16]{2,1,0:T(8,128)S(1)}, f32[16,16,16]{2,1,0:T(8,128)}, u32[]{:S(2)}) copy-start(f32[16,16,16]{2,1,0:T(8,128)} %copy-done.15) | copy-start | bytes 49156
  296.3 11.6 %copy-start.9 = (f32[1024,256]{0,1:T(8,128)S(1)}, f32[1024,256]{0,1:T(8,128)}, u32[]{:S(2)}) copy-start(f32[1024,256]{0,1:T(8,128)} %copy-done.8) | copy-start | bytes 3145732
  491.4 51.5 %copy-start.21 = (f32[16,256]{1,0:T(8,128)S(1)}, f32[16,256]{1,0:T(8,128)}, u32[]{:S(2)}) copy-start(f32[16,256]{1,0:T(8,128)} %get-tuple-element.414) | copy-start | bytes 49156
  491.4 51.6 %copy-start.20 = (f32[16,16]{1,0:T(8,128)S(1)}, f32[16,16]{1,0:T(8,128)}, u32[]{:S(2)}) copy-start(f32[16,16]{1,0:T(8,128)} %get-tuple-element.758) | copy-start | bytes 3076
  540.4 5.2 copy-start.1
  545.6 4.0 copy-start.18
  549.6 4.6 copy-start.2
  549.6 4.6 copy-start.4
  554.3 1.0 copy-start.6
  554.3 2.5 copy-start.22
  554.3 3.1 copy-start.13
  554.3 13.6 %copy-start.3 = (f32[1,1024,256]{1,2,0:T(8,128)S(1)}, f32[1,1024,256]{1,2,0:T(8,128)}, u32[]{:S(2)}) copy-start(f32[1,1024,256]{1,2,0:T(8,128)} %get-tuple-element.471) | copy-start | bytes 3145732
  554.3 13.6 %copy-start.5 = (f32[1,1024,256]{1,2,0:T(8,128)S(1)}, f32[1,1024,256]{1,2,0:T(8,128)}, u32[]{:S(2)}) copy-start(f32[1,1024,256]{1,2,0:T(8,128)} %get-tuple-element.472) | copy-start | bytes 3145732
  555.4 12.6 %collective-permute-start.1 = (f32[3,2,256]{1,2,0:T(8,128)S(1)}, f32[3,2,256]{1,2,0:T(8,128)S(1)}, u32[]{:S(2)}, u32[]{:S(2)}) collective-permute-start(f32[3,2,256]{1,2,0:T(8,128)S(1)} %slice.113), channel_id=1, source_target_pairs={{1,0},{2,1},{3,2},{4,3},{5,4},{6,5},{7,6},{8,7},{9,8},{10,9},{11,1... | collective-permute-start | bytes 18440 | tf_op jit(solution)/shard_map/ppermute | solution.py:13
  558.4 11.0 %copy-start.7 = (f32[1,1024,256]{1,2,0:T(8,128)S(1)}, f32[1,1024,256]{1,2,0:T(8,128)}, u32[]{:S(2)}) copy-start(f32[1,1024,256]{1,2,0:T(8,128)} %copy-done.6) | copy-start | bytes 3145732
  558.4 11.0 %copy-start.23 = (f32[3,256]{1,0:T(4,128)S(1)}, f32[3,256]{1,0:T(4,128)}, u32[]{:S(2)}) copy-start(f32[3,256]{1,0:T(4,128)} %get-tuple-element.499) | copy-start | bytes 9220
  558.4 11.0 %copy-start.24 = (f32[3,256]{1,0:T(4,128)S(1)}, f32[3,256]{1,0:T(4,128)}, u32[]{:S(2)}) copy-start(f32[3,256]{1,0:T(4,128)} %get-tuple-element.500) | copy-start | bytes 9220
  558.4 11.0 %copy-start.26 = (f32[3,1,256]{2,0,1:T(4,128)S(1)}, f32[3,1,256]{2,0,1:T(4,128)}, u32[]{:S(2)}) copy-start(f32[3,1,256]{2,0,1:T(4,128)} %copy-done.25) | copy-start | bytes 9220
where the time goes:
time: 580 us; the launch traced here: 575 us
  blocking collectives  211 us (36%)
  local copies, waits for them, and re-layouts  189 us (33%)
  matrix products  99.5 us (17%)
  other arithmetic  57.1 us (10%)
  waiting for transfers between devices  9.53 us (2%)
  starting transfers between devices  6.47 us (1%)
    psum x1, blocking collectives, per_device(): squares = lax.psum(jnp.sum(summed * summed), 'fsdp')  109 us
    dynamic_update_slice x16, local copies, waits for them, and re-layouts, per_device(): lax.scan(forward_block, (zero_state, zero_state, zero_pairs, zero_pairs,...  71.3 us
    psum x1, blocking collectives, per_device(): summed = lax.psum(filter_local, 'ctx')  61.1 us
    gather x2, local copies, waits for them, and re-layouts, per_device(): filter_taps[:, jnp.maximum(lag_index, 0)]  59.7 us
    all_gather x1, blocking collectives, per_device(): everyone = lax.all_gather(local_states[None], 'ctx', axis=0, tiled=True)  41.3 us
    dot_general x8, matrix products, forward_block(): jnp.einsum('kgnt,tgm->kngm', block_moments, e_block, precision=precise)  23.1 us
    dot_general x8, matrix products, forward_block(): jnp.einsum('tgm,sgm->gts', e_block, z_wide, precision=precise)  16.3 us
    unnamed x72, local copies, waits for them, and re-layouts  15.9 us
  transfers between devices with their start and end apart: 2, of which 1 were waited for; matrix products, arithmetic and copies ran while one was open for 14% of the time, Pallas kernels for 0%

commit v1 on v0

--- a/solution.py
+++ b/solution.py
@@ -65,24 +65,6 @@
     local_states = jnp.stack([end_states[0], end_states[1], start_state]).reshape(
         3, order_count, channels
     )
-    rate_cols = jnp.repeat(decay_rates.T, members, axis=1)
-    everyone = lax.all_gather(local_states[None], "ctx", axis=0, tiled=True)
-    device_ids = jnp.arange(ctx_count, dtype=jnp.int32)
-    ahead_steps = (ctx_index - 1 - device_ids).astype(jnp.float32)[:, None, None]
-    behind_steps = (device_ids - ctx_index - 1).astype(jnp.float32)[:, None, None]
-    ahead_weight = jnp.where(
-        ahead_steps >= 0, jnp.exp(-rate_cols[None] * (tokens * jnp.maximum(ahead_steps, 0.0))), 0.0
-    )
-    behind_weight = jnp.where(
-        behind_steps >= 0,
-        jnp.exp(-rate_cols[None] * (tokens * jnp.maximum(behind_steps, 0.0))),
-        0.0,
-    )
-    prev_state = jnp.sum(ahead_weight * everyone[:, 0], axis=0)
-    prev_lagged = jnp.sum(
-        ahead_weight * (everyone[:, 1] - tokens * ahead_steps * everyone[:, 0]), axis=0
-    )
-    next_state = jnp.sum(behind_weight * everyone[:, 2], axis=0)
     lag_axis = jnp.arange(block_len, dtype=jnp.float32)[None, None, :]
     block_pow = jnp.exp(-rate_axis * lag_axis)
     block_after = block_pow * jnp.exp(-rate_axis)
@@ -91,12 +73,15 @@
     block_ends = jnp.stack([jnp.flip(block_pow, 2), -jnp.flip(lag_axis * block_pow, 2)])
     coef_tail = mode_coefs[:, :, None] * jnp.flip(block_after, 2)
     block_span = jnp.exp(-decay_rates * block_len).T[:, :, None]
-    filter_taps = jnp.sum(mode_coefs[:, :, None] * block_pow, axis=1)
     lag_index = (
         jnp.arange(block_len, dtype=jnp.int32)[:, None]
         - jnp.arange(block_len, dtype=jnp.int32)[None, :]
     )
-    toeplitz = jnp.where(lag_index[None] >= 0, filter_taps[:, jnp.maximum(lag_index, 0)], 0.0)
+    lag_value = jnp.maximum(lag_index, 0).astype(jnp.float32)
+    pair_pow = jnp.exp(-decay_rates[:, :, None, None] * lag_value[None, None])
+    toeplitz = jnp.where(
+        lag_index[None] >= 0, jnp.sum(mode_coefs[:, :, None, None] * pair_pow, axis=1), 0.0
+    )
     z_blocks = grouped_z.reshape(block_count, block_len, group_count, members)
     e_blocks = grouped_e.reshape(block_count, block_len, group_count, members)
 
@@ -124,6 +109,54 @@
         (z_blocks, e_blocks),
     )
     first_acc, lag_acc, gram_acc = (final_carry[2], final_carry[3], final_carry[4])
+    lag_totals = diagonal_sums(gram_acc)
+    first_local = first_acc.T + jnp.sum(lag_totals[:, None, :] * block_pow, axis=2)
+    lag_local = lag_acc.T - jnp.sum(lag_totals[:, None, :] * lag_axis * block_pow, axis=2)
+    device_after = decay_from * jnp.exp(-rate_axis)
+    second_moment = jnp.einsum(
+        "gnt,tgm->ngm", (positions + 1.0) * device_after, grouped_e, precision=precise
+    )
+    partial_rows = jnp.stack([first_local, lag_local]).reshape(-1, channels)
+    partial_slot = jnp.zeros((order_count, channels), jnp.float32)
+    partial_slot = partial_slot.at[: partial_rows.shape[0]].set(partial_rows)
+    local_states = jnp.concatenate(
+        [local_states, second_moment.reshape(1, order_count, channels), partial_slot[None]]
+    )
+    rate_cols = jnp.repeat(decay_rates.T, members, axis=1)
+    everyone = lax.all_gather(local_states[None], "ctx", axis=0, tiled=True)
+    device_ids = jnp.arange(ctx_count, dtype=jnp.int32)
+    ahead_steps = (ctx_index - 1 - device_ids).astype(jnp.float32)[:, None, None]
+    behind_steps = (device_ids - ctx_index - 1).astype(jnp.float32)[:, None, None]
+    ahead_weight = jnp.where(
+        ahead_steps >= 0, jnp.exp(-rate_cols[None] * (tokens * jnp.maximum(ahead_steps, 0.0))), 0.0
+    )
+    behind_weight = jnp.where(
+        behind_steps >= 0,
+        jnp.exp(-rate_cols[None] * (tokens * jnp.maximum(behind_steps, 0.0))),
+        0.0,
+    )
+    prev_state = jnp.sum(ahead_weight * everyone[:, 0], axis=0)
+    next_state = jnp.sum(behind_weight * everyone[:, 2], axis=0)
+    all_ids = device_ids.astype(jnp.float32)
+    pair_steps = (all_ids[:, None] - 1.0 - all_ids[None, :])[:, :, None, None]
+    pair_weight = jnp.where(
+        pair_steps >= 0, jnp.exp(-rate_cols[None, None] * (tokens * jnp.maximum(pair_steps, 0.0))), 0.0
+    )
+    all_prev = jnp.sum(pair_weight * everyone[None, :, 0], axis=1)
+    all_lagged = jnp.sum(
+        pair_weight * (everyone[None, :, 1] - tokens * pair_steps * everyone[None, :, 0]), axis=1
+    )
+    all_first = jnp.exp(-rate_cols)[None] * everyone[:, 2]
+    cross_first = jnp.sum(all_first * all_prev, axis=0)
+    cross_lag = jnp.sum(all_first * all_lagged - everyone[:, 3] * all_prev, axis=0)
+    cross_first = cross_first.reshape(order_count, group_count, members).sum(axis=2).T
+    cross_lag = cross_lag.reshape(order_count, group_count, members).sum(axis=2).T
+    gathered_parts = everyone[:, 4, : partial_rows.shape[0]].reshape(
+        ctx_count, 2, group_count, order_count
+    )
+    local_totals = jnp.sum(gathered_parts, axis=0)
+    first_total = local_totals[0] + cross_first
+    lag_total = local_totals[1] + cross_lag
 
     def backward_block(later_state, e_block):
         inside_part = jnp.einsum("gts,tgm->sgm", toeplitz, e_block, precision=precise)
@@ -133,27 +166,14 @@
 
     top_state, grad_blocks = lax.scan(backward_block, zero_state, e_blocks, reverse=True)
     prev_grouped = prev_state.reshape(order_count, group_count, members)
-    lagged_grouped = prev_lagged.reshape(order_count, group_count, members)
     next_grouped = next_state.reshape(order_count, group_count, members)
-    device_after = decay_from * jnp.exp(-rate_axis)
     inner_sum = inner_blocks.reshape(tokens, group_count, members) + jnp.einsum(
         "gnt,ngm->tgm", mode_coefs[:, :, None] * device_after, prev_grouped, precision=precise
-    )
-    first_moment = jnp.exp(-decay_rates).T[:, :, None] * start_state
-    second_moment = jnp.einsum(
-        "gnt,tgm->ngm", (positions + 1.0) * device_after, grouped_e, precision=precise
-    )
-    first_acc = first_acc + jnp.sum(first_moment * prev_grouped, axis=2)
-    lag_acc = lag_acc + jnp.sum(
-        first_moment * lagged_grouped - second_moment * prev_grouped, axis=2
     )
     device_tail = mode_coefs[:, :, None] * jnp.flip(device_after, 2)
     product_grad = grad_blocks.reshape(tokens, group_count, members) + jnp.einsum(
         "gns,ngm->sgm", device_tail, next_grouped, precision=precise
     )
-    lag_totals = diagonal_sums(gram_acc)
-    first_total = first_acc.T + jnp.sum(lag_totals[:, None, :] * block_pow, axis=2)
-    lag_total = lag_acc.T - jnp.sum(lag_totals[:, None, :] * lag_axis * block_pow, axis=2)
     gain_part = jnp.sqrt(2.0 * decay_rates) * first_total
     rate_part = mode_coefs * (0.5 * first_total + decay_rates * lag_total)
     inner_flat = inner_sum.reshape(tokens, channels)
@@ -165,7 +185,7 @@
     feature_grads = short_conv(short_taps, appended, tokens, rim_rows, False).astype(jnp.bfloat16)
     filter_local = jnp.stack([gain_part, rate_part])
     entry_count = 2 * group_count * order_count * lax.axis_size("fsdp")
-    summed = lax.psum(filter_local, "ctx")
+    summed = filter_local
     squares = lax.psum(jnp.sum(summed * summed), "fsdp")
     factor = jnp.minimum(1.0, lax.rsqrt(squares / entry_count + 1e-06))
     clipped = summed * factor

time: 580 us -> 465 us (0.80)
  blocking collectives: 211 us -> 94.6 us
  local copies, waits for them, and re-layouts: 189 us -> 136 us
  waiting for transfers between devices: 9.53 us -> 39.2 us
  between operations: 1.78 us -> 15.4 us
  other arithmetic: 57.1 us -> 66.3 us
    psum x1 -> x0, blocking collectives: 61.1 us -> none  [per_device(): summed = lax.psum(filter_local, 'ctx')]
    gather x2 -> x0, local copies, waits for them, and re-layouts: 59.7 us -> none  [per_device(): filter_taps[:, jnp.maximum(lag_index, 0)]]
    all_gather x1 -> x0, blocking collectives: 41.3 us -> none  [per_device(): everyone = lax.all_gather(local_states[None], 'ctx', axis=0, tiled=True)]
    all_gather x0 -> x1, waiting for transfers between devices: none -> 30.7 us  [per_device(): everyone = lax.all_gather(local_states[None], 'ctx', axis=0, tiled=True)]
    psum x1, blocking collectives: 109 us -> 94.6 us  [per_device(): squares = lax.psum(jnp.sum(summed * summed), 'fsdp')]
    reduce_sum x3 -> x6, other arithmetic: 2.47 us -> 8.98 us  [the longest x1 5.16 us: per_device(): jnp.sum(mode_coefs[:, :, None, None] * pair_pow, axis=1)]
    unnamed x72 -> x96, local copies, waits for them, and re-layouts: 15.9 us -> 17.8 us
  transfers between devices with their start and end apart: 2 -> 3, of which waited for: 1 -> 2; matrix products, arithmetic and copies ran while one was open for 14% -> 21% of each run, Pallas kernels for 0% -> 0%
where the time goes in v1:
time: 465 us; the launch traced here: 461 us
  local copies, waits for them, and re-layouts  136 us (29%)
  matrix products  103 us (22%)
  blocking collectives  94.6 us (20%)
  other arithmetic  66.3 us (14%)
  waiting for transfers between devices  39.2 us (8%)
  between operations  15.4 us (3%)
  starting transfers between devices  6.51 us (1%)
    psum x1, blocking collectives, per_device(): squares = lax.psum(jnp.sum(summed * summed), 'fsdp')  94.6 us
    dynamic_update_slice x16, local copies, waits for them, and re-layouts, per_device(): lax.scan(forward_block, (zero_state, zero_state, zero_pairs, zero_pairs,...  71.2 us
    all_gather x1, waiting for transfers between devices, per_device(): everyone = lax.all_gather(local_states[None], 'ctx', axis=0, tiled=True)  30.7 us
    dot_general x8, matrix products, forward_block(): jnp.einsum('kgnt,tgm->kngm', block_moments, e_block, precision=precise)  23.1 us
    unnamed x96, local copies, waits for them, and re-layouts  17.8 us
    dot_general x8, matrix products, forward_block(): jnp.einsum('tgm,sgm->gts', e_block, z_wide, precision=precise)  16.3 us
    dot_general x8, matrix products, forward_block(): jnp.einsum('kgns,sgm->kngm', block_ends, z_wide, precision=threepass)  13.8 us
    reduce_sum x8, other arithmetic, forward_block(): jnp.sum(moments[0] * lagged - moments[1] * mode_state, axis=2)  13.1 us
  transfers between devices with their start and end apart: 3, of which 2 were waited for; matrix products, arithmetic and copies ran while one was open for 21% of the time, Pallas kernels for 0%

profile of v1, /device:TPU:1, one launch (start us, length us, event | category | flops | bytes accessed | tf_op | source)
XLA Modules:
  0.0 461.2 jit_solution(7824403788756353742)
XLA Ops:
  8.8 5.1 %collective-permute-start = (bf16[3,2,256]{1,2,0:T(8,128)(2,1)}, bf16[3,2,256]{1,2,0:T(8,128)(2,1)}, u32[]{:S(2)}, u32[]{:S(2)}) collective-permute-start(bf16[3,2,256]{1,2,0:T(8,128)(2,1)} %copy.110), channel_id=1, source_target_pairs={{0,1},{1,2},{2,3},{3,4},{4,5},{5,6},{6,7},{7,8},{8,9},{9,10},{10,1... | collective-permute-start | bytes 9224 | tf_op jit(solution)/shard_map/ppermute | solution.py:13
  28.5 5.2 %multiply_reduce_fusion.1 = f32[16,128,128]{2,1,0:T(8,128)S(1)} fusion(f32[128,128]{1,0:T(8,128)S(1)} %maximum_convert_fusion, f32[16,16]{1,0:T(8,128)S(1)} %get-tuple-element.800, f32[16,16]{1,0:T(8,128)} %copy.115), kind=kLoop, calls=%fused_computation.65 | loop fusion | flops 12320768 | bytes 1116160 | tf_op jit(solution)/shard_map/reduce_sum | solution.py:83
  37.1 2.6 copy.109
  42.0 2.0 copy.112
  44.0 5.5 %rev.26 = f32[16,16,1024]{2,1,0:T(8,128)} reverse(f32[16,16,1024]{2,1,0:T(8,128)} %get-tuple-element.565), dimensions={2} | reverse | bytes 2097152 | tf_op jit(solution)/shard_map/jit(_flip)/rev | solution.py:60
  53.0 3.3 rev.30
  56.4 4.6 %multiply_add_fusion = f32[3,1024,256]{1,2,0:T(8,128)S(1)} fusion(bf16[3,1024,256]{1,2,0:T(8,128)(2,1)} %copy.109, bf16[3,2,256]{1,2,0:T(8,128)(2,1)} %collective-permute-done, f32[3,256]{1,0:T(4,128)} %get-tuple-element.575, f32[3,256]{1,0:T(4,128)} %get-tuple-element.576, f32[3,256]{1,0:T(4,128)} %bitcast.282), kind=kLoop, calls=%fused_computation.76 | loop fusion | flops 11010048 | bytes 4730880 | tf_op jit(solution)/shard_map/add | solution.py:32
  66.1 134.3 %while.39 = (s32[]{:T(128)}, f32[16,16,16]{0,2,1:T(8,128)}, f32[16,16,16]{0,2,1:T(8,128)}, f32[16,16]{0,1:T(8,128)}, f32[16,16]{0,1:T(8,128)}, /*index=5*/f32[16...) while((s32[]{:T(128)}, f32[16,16,16]{0,2,1:T(8,128)}, ...), condition=%wide.region_4.5_spmd.clone, body=%wide.region_1.4_spmd.clone.sunk | while | flops 101380864 | bytes 5014714 | solution.py:106
  68.9 2.9 convolution_bitcast_fusion.7
  74.7 4.5 dynamic_update_slice.17
  84.3 2.9 convolution_bitcast_fusion.7
  91.7 4.5 dynamic_update_slice.17
  101.3 2.9 convolution_bitcast_fusion.7
  108.7 4.5 dynamic_update_slice.17
  118.3 2.9 convolution_bitcast_fusion.7
  125.8 4.5 dynamic_update_slice.17
  135.3 2.9 convolution_bitcast_fusion.7
  142.8 4.5 dynamic_update_slice.17
  152.4 2.9 convolution_bitcast_fusion.7
  159.8 4.5 dynamic_update_slice.17
  169.4 2.9 convolution_bitcast_fusion.7
  176.9 4.5 dynamic_update_slice.17
  186.4 2.9 convolution_bitcast_fusion.7
  193.9 4.5 dynamic_update_slice.17
  200.4 5.8 %rev.28 = f32[16,128,128]{2,1,0:T(8,128)} reverse(f32[16,128,128]{2,1,0:T(8,128)S(1)} %get-tuple-element.253), dimensions={2} | reverse | bytes 2097152 | tf_op jit(solution)/shard_map/jit(_flip)/rev | solution.py:18
  210.3 6.2 %reshape.321 = f32[16,128,255]{2,1,0:T(8,128)} reshape(f32[16,32640]{1,0:T(8,128)} %slice.145) | data formatting | bytes 4177920 | tf_op jit(solution)/shard_map/reshape | solution.py:23
  221.4 5.0 %fusion.63 = f32[2,16,16,16]{1,3,0,2:T(8,128)} fusion(bf16[1024,16,16,1]{0,2,3,1:T(8,128)(2,1)} %bitcast.272, f32[1,16,16,1024]{3,2,0,1:T(8,128)} %negate_bitcast_fusion, f32[1,16,16,1024]{3,2,0,1:T(8,128)} %bitcast.269), kind=kOutput, calls=%fused_computation.91 | convolution fusion | flops 50855936 | bytes 2654208 | tf_op jit(solution)/shard_map/kgns,sgm->kngm/dot_general | solution.py:61
  231.3 2.9 fusion.70
  238.5 48.9 %while.40 = (s32[]{:T(128)}, f32[16,16,16]{0,2,1:T(8,128)S(1)}, f32[8,128,16,16]{1,0,3,2:T(8,128)}, f32[16,16,1]{0,1,2:T(8,128)S(1)}, f32[8,128,16,16]{1,3,2,0:T...) while((s32[]{:T(128)}, f32[16,16,16]{0,2,1:T(8,128)S(1)}, ...), condition=%wide.region_10.11_spmd.clone, body=%wide.region_9.10_spmd.clone.sunk | while | flops 62996484 | bytes 2277520 | solution.py:167
  239.7 4.4 dynamic_update_slice.18
  245.8 4.4 dynamic_update_slice.18
  251.9 4.4 dynamic_update_slice.18
  258.0 4.4 dynamic_update_slice.18
  264.2 4.4 dynamic_update_slice.18
  270.3 4.4 dynamic_update_slice.18
  276.4 4.4 dynamic_update_slice.18
  282.5 4.4 dynamic_update_slice.18
  287.5 2.4 reshape.324
  289.9 30.7 %all-gather.3.cloned.1.call-done = f32[80,16,256]{2,1,0:T(8,128)} async-done(((f32[5,16,256]{2,1,0:T(8,128)}), f32[80,16,256]{2,1,0:T(8,128)}) %all-gather.3.cloned.1.call-update) | async-done | bytes 1310736 | tf_op jit(solution)/shard_map/all_gather | solution.py:126
  322.7 2.4 multiply_reduce_fusion.2
  326.8 2.4 reshape.317
  329.2 94.6 %psum.7 = f32[]{:T(128)} all-reduce(f32[]{:T(128)} %multiply_reduce_fusion.9), channel_id=1, replica_groups=mesh['fsdp'=32,'ctx'=16] {'fsdp'}, use_global_device_ids=true, to_apply=%region_20.21 | all-reduce | flops 1 | bytes 8 | tf_op jit(solution)/shard_map/psum | solution.py:189
  424.7 2.6 fusion.61
  429.0 2.6 fusion.62
  431.6 2.0 fusion.66
  438.5 8.5 %collective-permute-done.1 = f32[3,2,256]{1,2,0:T(8,128)S(1)} collective-permute-done((f32[3,2,256]{1,2,0:T(8,128)S(1)}, f32[3,2,256]{1,2,0:T(8,128)S(1)}, u32[]{:S(2)}, u32[]{:S(2)}) %collective-permute-start.1) | collective-permute-done | bytes 6176 | tf_op jit(solution)/shard_map/ppermute | solution.py:13
  448.5 3.3 fusion.54
  451.8 2.6 copy.139
  (259 shorter events, 148.7 us)
Async XLA Ops:
  7.2 17.1 %copy-start.34 = (f32[3,3,256]{2,1,0:T(4,128)S(1)}, f32[3,3,256]{2,1,0:T(4,128)}, u32[]{:S(2)}) copy-start(f32[3,3,256]{2,1,0:T(4,128)} %param.12) | copy-start | bytes 27652
  7.2 17.7 %copy-start.31 = (f32[16,16]{1,0:T(8,128)S(1)}, f32[16,16]{1,0:T(8,128)}, u32[]{:S(2)}) copy-start(f32[16,16]{1,0:T(8,128)} %param.14) | copy-start | bytes 3076
  7.2 313.4 %all-gather.3.cloned.1.call-start = ((), (), s32[]{:S(2)}) async-start(), calls=%async_computation | async-start | bytes 1392640 | tf_op jit(solution)/shard_map/all_gather | solution.py:126
  8.8 47.6 %collective-permute-start = (bf16[3,2,256]{1,2,0:T(8,128)(2,1)}, bf16[3,2,256]{1,2,0:T(8,128)(2,1)}, u32[]{:S(2)}, u32[]{:S(2)}) collective-permute-start(bf16[3,2,256]{1,2,0:T(8,128)(2,1)} %copy.110), channel_id=1, source_target_pairs={{0,1},{1,2},{2,3},{3,4},{4,5},{5,6},{6,7},{7,8},{8,9},{9,10},{10,1... | collective-permute-start | bytes 9224 | tf_op jit(solution)/shard_map/ppermute | solution.py:13
  15.9 9.7 %copy-start.18 = (f32[16,16]{0,1:T(8,128)}, f32[16,16]{0,1:T(8,128)S(1)}, u32[]{:S(2)}) copy-start(f32[16,16]{0,1:T(8,128)S(1)} %copy.113) | copy-start | bytes 3076
  24.9 0.7 copy-start.20
  28.4 6.1 %copy-start.13 = (f32[1,16,16,128]{3,2,1,0:T(8,128)S(1)}, f32[1,16,16,128]{3,2,1,0:T(8,128)}, u32[]{:S(2)}) copy-start(f32[1,16,16,128]{3,2,1,0:T(8,128)} %negate_bitcast_fusion.1) | copy-start | bytes 393220
  28.4 6.0 %copy-start.14 = (f32[16,16,128]{2,1,0:T(8,128)S(1)}, f32[16,16,128]{2,1,0:T(8,128)}, u32[]{:S(2)}) copy-start(f32[16,16,128]{2,1,0:T(8,128)} %rev.24) | copy-start | bytes 393220
  28.4 6.8 %copy-start.15 = (f32[1,16,16,128]{3,2,0,1:T(8,128)S(1)}, f32[1,16,16,128]{3,2,0,1:T(8,128)}, u32[]{:S(2)}) copy-start(f32[1,16,16,128]{3,2,0,1:T(8,128)} %get-tuple-element.558) | copy-start | bytes 393220
  28.4 6.8 %copy-start.16 = (f32[1,16,16,128]{3,2,0,1:T(8,128)S(1)}, f32[1,16,16,128]{3,2,0,1:T(8,128)}, u32[]{:S(2)}) copy-start(f32[1,16,16,128]{3,2,0,1:T(8,128)} %get-tuple-element.559) | copy-start | bytes 393220
  28.4 7.5 %copy-start.29 = (f32[3,1,256]{2,1,0:T(1,128)S(1)}, f32[3,1,256]{2,1,0:T(1,128)}, u32[]{:S(2)}) copy-start(f32[3,1,256]{2,1,0:T(1,128)} %get-tuple-element.561) | copy-start | bytes 9220
  28.4 7.5 %copy-start.30 = (f32[3,1,256]{2,1,0:T(1,128)S(1)}, f32[3,1,256]{2,1,0:T(1,128)}, u32[]{:S(2)}) copy-start(f32[3,1,256]{2,1,0:T(1,128)} %get-tuple-element.562) | copy-start | bytes 9220
  28.4 8.1 %copy-start.23 = (pred[128,128]{1,0:T(8,128)(4,1)S(1)}, pred[128,128]{1,0:T(8,128)(4,1)}, u32[]{:S(2)}) copy-start(pred[128,128]{1,0:T(8,128)(4,1)} %fusion.89) | copy-start | bytes 49156
  35.2 6.2 %copy-start.28 = (f32[3,1,256]{2,1,0:T(1,128)S(1)}, f32[3,1,256]{2,1,0:T(1,128)}, u32[]{:S(2)}) copy-start(f32[3,1,256]{2,1,0:T(1,128)} %get-tuple-element.560) | copy-start | bytes 9220
  37.1 12.4 %copy-start.27 = (f32[16,16]{0,1:T(8,128)S(1)}, f32[16,16]{0,1:T(8,128)}, u32[]{:S(2)}) copy-start(f32[16,16]{0,1:T(8,128)} %get-tuple-element.569) | copy-start | bytes 3076
  61.0 1.8 copy-start
  61.0 1.4 copy-start.10
  62.8 1.0 copy-start.8
  216.5 13.3 %copy-start.9 = (f32[1024,256]{0,1:T(8,128)S(1)}, f32[1024,256]{0,1:T(8,128)}, u32[]{:S(2)}) copy-start(f32[1024,256]{0,1:T(8,128)} %copy-done.8) | copy-start | bytes 3145732
  287.4 35.3 %copy-start.17 = (f32[16,256]{1,0:T(8,128)S(1)}, f32[16,256]{1,0:T(8,128)}, u32[]{:S(2)}) copy-start(f32[16,256]{1,0:T(8,128)} %neg.43) | copy-start | bytes 49156
  287.4 35.3 %copy-start.32 = (f32[16,16]{1,0:T(8,128)S(1)}, f32[16,16]{1,0:T(8,128)}, u32[]{:S(2)}) copy-start(f32[16,16]{1,0:T(8,128)} %get-tuple-element.573) | copy-start | bytes 3076
  287.4 35.3 %copy-start.33 = (f32[16,16]{1,0:T(8,128)S(1)}, f32[16,16]{1,0:T(8,128)}, u32[]{:S(2)}) copy-start(f32[16,16]{1,0:T(8,128)} %get-tuple-element.574) | copy-start | bytes 3076
  287.4 35.3 %copy-start.39 = (pred[16,16]{1,0:T(8,128)(4,1)S(1)}, pred[16,16]{1,0:T(8,128)(4,1)}, u32[]{:S(2)}) copy-start(pred[16,16]{1,0:T(8,128)(4,1)} %subtract_compare_fusion) | copy-start | bytes 772
  287.4 37.7 %copy-start.22 = (f32[16,256]{1,0:T(8,128)S(1)}, f32[16,256]{1,0:T(8,128)}, u32[]{:S(2)}) copy-start(f32[16,256]{1,0:T(8,128)} %exp.54) | copy-start | bytes 49156
  287.4 37.7 %copy-start.35 = (f32[16]{0:T(128)S(1)}, f32[16]{0:T(128)}, u32[]{:S(2)}) copy-start(f32[16]{0:T(128)} %get-tuple-element.577) | copy-start | bytes 196
  287.4 37.7 %copy-start.36 = (f32[16]{0:T(128)S(1)}, f32[16]{0:T(128)}, u32[]{:S(2)}) copy-start(f32[16]{0:T(128)} %get-tuple-element.578) | copy-start | bytes 196
  287.4 37.7 %copy-start.37 = (pred[16]{0:T(512)(128)(4,1)S(1)}, pred[16]{0:T(512)(128)(4,1)}, u32[]{:S(2)}) copy-start(pred[16]{0:T(512)(128)(4,1)} %get-tuple-element.579) | copy-start | bytes 52
  287.4 37.7 %copy-start.38 = (pred[16]{0:T(512)(128)(4,1)S(1)}, pred[16]{0:T(512)(128)(4,1)}, u32[]{:S(2)}) copy-start(pred[16]{0:T(512)(128)(4,1)} %get-tuple-element.580) | copy-start | bytes 52
  287.5 38.7 %copy-start.19 = (f32[16,16]{0,1:T(8,128)S(1)}, f32[16,16]{0,1:T(8,128)}, u32[]{:S(2)}) copy-start(f32[16,16]{0,1:T(8,128)} %copy-done.18) | copy-start | bytes 3076
  287.5 38.7 %copy-start.21 = (f32[16,16]{0,1:T(8,128)S(1)}, f32[16,16]{0,1:T(8,128)}, u32[]{:S(2)}) copy-start(f32[16,16]{0,1:T(8,128)} %copy-done.20) | copy-start | bytes 3076
  320.5 4.6 %copy-start.12 = (f32[80,16,256]{2,1,0:T(8,128)S(1)}, f32[80,16,256]{2,1,0:T(8,128)}, u32[]{:S(2)}) copy-start(f32[80,16,256]{2,1,0:T(8,128)} %all-gather.3.cloned.1.call-done) | copy-start | bytes 3932164
  325.4 101.9 %copy-start.1 = (f32[3,1024,256]{1,2,0:T(8,128)S(1)}, f32[3,1024,256]{1,2,0:T(8,128)}, u32[]{:S(2)}) copy-start(f32[3,1024,256]{1,2,0:T(8,128)} %copy-done) | copy-start | bytes 9437188
  429.0 4.7 %copy-start.2 = (f32[1,1024,256]{1,2,0:T(8,128)S(1)}, f32[1,1024,256]{1,2,0:T(8,128)}, u32[]{:S(2)}) copy-start(f32[1,1024,256]{1,2,0:T(8,128)} %get-tuple-element.546) | copy-start | bytes 3145732
  429.0 4.7 %copy-start.4 = (f32[1,1024,256]{1,2,0:T(8,128)S(1)}, f32[1,1024,256]{1,2,0:T(8,128)}, u32[]{:S(2)}) copy-start(f32[1,1024,256]{1,2,0:T(8,128)} %get-tuple-element.547) | copy-start | bytes 3145732
  433.7 1.0 copy-start.6
  433.7 3.8 copy-start.11
  433.7 13.3 %copy-start.3 = (f32[1,1024,256]{1,2,0:T(8,128)S(1)}, f32[1,1024,256]{1,2,0:T(8,128)}, u32[]{:S(2)}) copy-start(f32[1,1024,256]{1,2,0:T(8,128)} %get-tuple-element.546) | copy-start | bytes 3145732
  433.7 13.3 %copy-start.5 = (f32[1,1024,256]{1,2,0:T(8,128)S(1)}, f32[1,1024,256]{1,2,0:T(8,128)}, u32[]{:S(2)}) copy-start(f32[1,1024,256]{1,2,0:T(8,128)} %get-tuple-element.547) | copy-start | bytes 3145732
  434.8 12.3 %collective-permute-start.1 = (f32[3,2,256]{1,2,0:T(8,128)S(1)}, f32[3,2,256]{1,2,0:T(8,128)S(1)}, u32[]{:S(2)}, u32[]{:S(2)}) collective-permute-start(f32[3,2,256]{1,2,0:T(8,128)S(1)} %slice.149), channel_id=1, source_target_pairs={{1,0},{2,1},{3,2},{4,3},{5,4},{6,5},{7,6},{8,7},{9,8},{10,9},{11,1... | collective-permute-start | bytes 18440 | tf_op jit(solution)/shard_map/ppermute | solution.py:13
  438.5 10.0 %copy-start.7 = (f32[1,1024,256]{1,2,0:T(8,128)S(1)}, f32[1,1024,256]{1,2,0:T(8,128)}, u32[]{:S(2)}) copy-start(f32[1,1024,256]{1,2,0:T(8,128)} %copy-done.6) | copy-start | bytes 3145732
  438.5 10.0 %copy-start.24 = (f32[3,256]{1,0:T(4,128)S(1)}, f32[3,256]{1,0:T(4,128)}, u32[]{:S(2)}) copy-start(f32[3,256]{1,0:T(4,128)} %get-tuple-element.575) | copy-start | bytes 9220
  438.5 10.0 %copy-start.25 = (f32[3,256]{1,0:T(4,128)S(1)}, f32[3,256]{1,0:T(4,128)}, u32[]{:S(2)}) copy-start(f32[3,256]{1,0:T(4,128)} %get-tuple-element.576) | copy-start | bytes 9220
  438.5 10.0 %copy-start.26 = (f32[3,1,256]{2,0,1:T(4,128)S(1)}, f32[3,1,256]{2,0,1:T(4,128)}, u32[]{:S(2)}) copy-start(f32[3,1,256]{2,0,1:T(4,128)} %copy.183) | copy-start | bytes 9220
Sparse Core Ops, SparseCore 0:
  237.5 83.0 all-gather.2

commit v2 on v1

--- a/solution.py
+++ b/solution.py
@@ -1,10 +1,63 @@
 import jax
 import jax.numpy as jnp
 from jax import lax
+from jax.experimental import pallas as pl
+from jax.experimental.pallas import tpu as pltpu
 from jax.sharding import PartitionSpec as P
+import functools
+
+MESH = pl.DeviceIdType.MESH
 
 precise = lax.Precision.HIGHEST
 threepass = lax.Precision.HIGH
+
+
+def gather_kernel(axis, count, x_ref, o_ref, held, send_sem, recv_sem):
+    me = lax.axis_index(axis)
+
+    def device(peer):
+        if axis == "ctx":
+            return (lax.axis_index("fsdp"), peer)
+        return (peer, lax.axis_index("ctx"))
+
+    barrier = pltpu.get_barrier_semaphore()
+    for step in range(1, count):
+        pl.semaphore_signal(
+            barrier, inc=1, device_id=device(lax.rem(me + step, count)), device_id_type=MESH
+        )
+    pl.semaphore_wait(barrier, count - 1)
+    copies = []
+    for step in range(1, count):
+        copy = pltpu.make_async_remote_copy(
+            src_ref=x_ref,
+            dst_ref=held.at[me],
+            send_sem=send_sem.at[step - 1],
+            recv_sem=recv_sem.at[step - 1],
+            device_id=device(lax.rem(me + step, count)),
+            device_id_type=MESH,
+        )
+        copy.start()
+        copies.append(copy)
+    for copy in copies:
+        copy.wait()
+    held[me] = x_ref[...]
+    o_ref[...] = held[...]
+
+
+def gather_along(value, axis, collective_id):
+    count = lax.axis_size(axis)
+    return pl.pallas_call(
+        functools.partial(gather_kernel, axis, count),
+        out_shape=jax.ShapeDtypeStruct((count,) + value.shape, value.dtype),
+        in_specs=[pl.BlockSpec(memory_space=pltpu.VMEM)],
+        out_specs=pl.BlockSpec(memory_space=pltpu.VMEM),
+        scratch_shapes=[
+            pltpu.VMEM((count,) + value.shape, value.dtype),
+            pltpu.SemaphoreType.DMA((count - 1,)),
+            pltpu.SemaphoreType.DMA((count - 1,)),
+        ],
+        compiler_params=pltpu.CompilerParams(collective_id=collective_id, has_side_effects=True),
+    )(value)
 
 
 def passed_along(value, axis, steps):
@@ -123,7 +176,7 @@
         [local_states, second_moment.reshape(1, order_count, channels), partial_slot[None]]
     )
     rate_cols = jnp.repeat(decay_rates.T, members, axis=1)
-    everyone = lax.all_gather(local_states[None], "ctx", axis=0, tiled=True)
+    everyone = gather_along(local_states, "ctx", 0)
     device_ids = jnp.arange(ctx_count, dtype=jnp.int32)
     ahead_steps = (ctx_index - 1 - device_ids).astype(jnp.float32)[:, None, None]
     behind_steps = (device_ids - ctx_index - 1).astype(jnp.float32)[:, None, None]
@@ -186,7 +239,8 @@
     filter_local = jnp.stack([gain_part, rate_part])
     entry_count = 2 * group_count * order_count * lax.axis_size("fsdp")
     summed = filter_local
-    squares = lax.psum(jnp.sum(summed * summed), "fsdp")
+    square_tile = jnp.full((8, 128), jnp.sum(summed * summed), jnp.float32)
+    squares = jnp.sum(gather_along(square_tile, "fsdp", 1)[:, 0, 0])
     factor = jnp.minimum(1.0, lax.rsqrt(squares / entry_count + 1e-06))
     clipped = summed * factor
     return (mixer_output, feature_grads, clipped[0], clipped[1])

time: 465 us -> 393 us (0.85)
  blocking collectives: 94.6 us -> 0 us
  Pallas kernels: 0 us -> 59.3 us
  waiting for transfers between devices: 39.2 us -> 11.7 us
  between operations: 15.4 us -> 1.96 us
  other arithmetic: 66.3 us -> 71.3 us
    psum x1 -> x0, blocking collectives: 94.6 us -> none  [per_device(): squares = lax.psum(jnp.sum(summed * summed), 'fsdp')]
    pallas_call x0 -> x2, Pallas kernels: none -> 59.3 us  [gather_along(): pl.pallas_call(functools.partial(gather_kernel, axis, count), out_shape=j...]
    all_gather x1 -> x0, waiting for transfers between devices: 30.7 us -> none  [per_device(): everyone = lax.all_gather(local_states[None], 'ctx', axis=0, tiled=True)]
    unnamed x96 -> x84, local copies, waits for them, and re-layouts: 17.8 us -> 13.8 us
  transfers between devices with their start and end apart: 3 -> 2, of which waited for: 2 -> 1; matrix products, arithmetic and copies ran while one was open for 21% -> 10% of each run, Pallas kernels for 0% -> 0%
where the time goes in v2:
time: 393 us; the launch traced here: 388 us
  local copies, waits for them, and re-layouts  134 us (34%)
  matrix products  103 us (26%)
  other arithmetic  71.3 us (18%)
  Pallas kernels  59.3 us (15%)
  waiting for transfers between devices  11.7 us (3%)
  starting transfers between devices  6.47 us (2%)
    dynamic_update_slice x16, local copies, waits for them, and re-layouts, per_device(): lax.scan(forward_block, (zero_state, zero_state, zero_pairs, zero_pairs,...  71.3 us
    pallas_call x2, Pallas kernels, gather_along(): pl.pallas_call(functools.partial(gather_kernel, axis, count), out_shape=j...  59.3 us
    dot_general x8, matrix products, forward_block(): jnp.einsum('kgnt,tgm->kngm', block_moments, e_block, precision=precise)  23.1 us
    dot_general x8, matrix products, forward_block(): jnp.einsum('tgm,sgm->gts', e_block, z_wide, precision=precise)  16.3 us
    unnamed x84, local copies, waits for them, and re-layouts  13.8 us
    dot_general x8, matrix products, forward_block(): jnp.einsum('kgns,sgm->kngm', block_ends, z_wide, precision=threepass)  13.8 us
    reduce_sum x8, other arithmetic, forward_block(): jnp.sum(moments[0] * lagged - moments[1] * mode_state, axis=2)  13 us
    dot_general x8, matrix products, forward_block(): jnp.einsum('gts,sgm->tgm', toeplitz, z_wide, precision=threepass)  11.9 us
  transfers between devices with their start and end apart: 2, of which 1 were waited for; matrix products, arithmetic and copies ran while one was open for 10% of the time, Pallas kernels for 0%

profile of v2, /device:TPU:1, one launch (start us, length us, event | category | flops | bytes accessed | tf_op | source)
XLA Modules:
  0.0 388.2 jit_solution(133738629976029621)
XLA Ops:
  2.2 5.0 %collective-permute-start = (bf16[3,2,256]{1,2,0:T(8,128)(2,1)}, bf16[3,2,256]{1,2,0:T(8,128)(2,1)}, u32[]{:S(2)}, u32[]{:S(2)}) collective-permute-start(bf16[3,2,256]{1,2,0:T(8,128)(2,1)} %copy.114), channel_id=1, source_target_pairs={{0,1},{1,2},{2,3},{3,4},{4,5},{5,6},{6,7},{7,8},{8,9},{9,10},{10,1... | collective-permute-start | bytes 9224 | tf_op jit(solution)/shard_map/ppermute | solution.py:66
  10.8 2.3 fusion.72
  21.0 5.1 %multiply_reduce_fusion.1 = f32[16,128,128]{2,1,0:T(8,128)S(1)} fusion(f32[128,128]{1,0:T(8,128)S(1)} %maximum_convert_fusion, f32[16,16]{1,0:T(8,128)S(1)} %get-tuple-element.800, f32[16,16]{1,0:T(8,128)} %copy.119), kind=kLoop, calls=%fused_computation.65 | loop fusion | flops 12320768 | bytes 1116160 | tf_op jit(solution)/shard_map/reduce_sum | solution.py:136
  33.1 5.7 %rev.26 = f32[16,16,1024]{2,1,0:T(8,128)} reverse(f32[16,16,1024]{2,1,0:T(8,128)} %get-tuple-element.565), dimensions={2} | reverse | bytes 2097152 | tf_op jit(solution)/shard_map/jit(_flip)/rev | solution.py:113
  39.7 5.6 %rev.30 = f32[16,16,1024]{2,1,0:T(8,128)} reverse(f32[16,16,1024]{2,1,0:T(8,128)} %get-tuple-element.563), dimensions={2} | reverse | bytes 2097152 | tf_op jit(solution)/shard_map/jit(_flip)/rev | solution.py:226
  45.3 4.8 %multiply_add_fusion = f32[3,1024,256]{1,2,0:T(8,128)S(1)} fusion(bf16[3,1024,256]{1,2,0:T(8,128)(2,1)} %copy.113, bf16[3,2,256]{1,2,0:T(8,128)(2,1)} %collective-permute-done, f32[3,256]{1,0:T(4,128)S(1)} %copy-done.23, f32[3,256]{1,0:T(4,128)S(1)} %copy-done.25, f32[3,256]{1,0:T(4,128)S(1)} %bitcast.273), kind=kLoop, calls=%fused_computation.76 | loop fusion | flops 11010048 | bytes 4730880 | tf_op jit(solution)/shard_map/add | solution.py:85
  54.4 134.2 %while.39 = (s32[]{:T(128)}, f32[16,16,16]{0,2,1:T(8,128)}, f32[16,16,16]{0,2,1:T(8,128)}, f32[16,16]{0,1:T(8,128)}, f32[16,16]{0,1:T(8,128)}, /*index=5*/f32[16...) while((s32[]{:T(128)}, f32[16,16,16]{0,2,1:T(8,128)}, ...), condition=%wide.region_4.5_spmd.clone, body=%wide.region_1.4_spmd.clone.sunk | while | flops 101380864 | bytes 5014714 | solution.py:159
  57.2 2.9 convolution_bitcast_fusion.7
  63.0 4.5 %dynamic_update_slice.17 = f32[8,128,16,16]{1,0,3,2:T(8,128)} dynamic-update-slice(f32[8,128,16,16]{1,0,3,2:T(8,128)} %get-tuple-element.763, f32[1,128,16,16]{1,0,3,2:T(1,128)S(1)} %bitcast.255, s32[]{:T(128)} %get-tuple-element.757, s32[]{:T(128)} %constant.108.clone.1..sunk, s32[]{:T(128)} %constant.108.clone.1..sunk, s32[]{:T(128)} %constant.108.clone.1..sunk) | dynamic-update-slice | bytes 262148 | tf_op jit(solution)/shard_map/while/body/jit(dynamic_update_index_in_dim)/dynamic_update_slice | solution.py:159
  72.6 2.9 convolution_bitcast_fusion.7
  80.0 4.5 %dynamic_update_slice.17 = f32[8,128,16,16]{1,0,3,2:T(8,128)} dynamic-update-slice(f32[8,128,16,16]{1,0,3,2:T(8,128)} %get-tuple-element.763, f32[1,128,16,16]{1,0,3,2:T(1,128)S(1)} %bitcast.255, s32[]{:T(128)} %get-tuple-element.757, s32[]{:T(128)} %constant.108.clone.1..sunk, s32[]{:T(128)} %constant.108.clone.1..sunk, s32[]{:T(128)} %constant.108.clone.1..sunk) | dynamic-update-slice | bytes 262148 | tf_op jit(solution)/shard_map/while/body/jit(dynamic_update_index_in_dim)/dynamic_update_slice | solution.py:159
  84.5 2.0 convolution_add_fusion.6
  89.6 2.9 convolution_bitcast_fusion.7
  97.0 4.5 %dynamic_update_slice.17 = f32[8,128,16,16]{1,0,3,2:T(8,128)} dynamic-update-slice(f32[8,128,16,16]{1,0,3,2:T(8,128)} %get-tuple-element.763, f32[1,128,16,16]{1,0,3,2:T(1,128)S(1)} %bitcast.255, s32[]{:T(128)} %get-tuple-element.757, s32[]{:T(128)} %constant.108.clone.1..sunk, s32[]{:T(128)} %constant.108.clone.1..sunk, s32[]{:T(128)} %constant.108.clone.1..sunk) | dynamic-update-slice | bytes 262148 | tf_op jit(solution)/shard_map/while/body/jit(dynamic_update_index_in_dim)/dynamic_update_slice | solution.py:159
  106.6 2.9 convolution_bitcast_fusion.7
  114.1 4.5 %dynamic_update_slice.17 = f32[8,128,16,16]{1,0,3,2:T(8,128)} dynamic-update-slice(f32[8,128,16,16]{1,0,3,2:T(8,128)} %get-tuple-element.763, f32[1,128,16,16]{1,0,3,2:T(1,128)S(1)} %bitcast.255, s32[]{:T(128)} %get-tuple-element.757, s32[]{:T(128)} %constant.108.clone.1..sunk, s32[]{:T(128)} %constant.108.clone.1..sunk, s32[]{:T(128)} %constant.108.clone.1..sunk) | dynamic-update-slice | bytes 262148 | tf_op jit(solution)/shard_map/while/body/jit(dynamic_update_index_in_dim)/dynamic_update_slice | solution.py:159
  123.6 2.9 convolution_bitcast_fusion.7
  131.1 4.5 %dynamic_update_slice.17 = f32[8,128,16,16]{1,0,3,2:T(8,128)} dynamic-update-slice(f32[8,128,16,16]{1,0,3,2:T(8,128)} %get-tuple-element.763, f32[1,128,16,16]{1,0,3,2:T(1,128)S(1)} %bitcast.255, s32[]{:T(128)} %get-tuple-element.757, s32[]{:T(128)} %constant.108.clone.1..sunk, s32[]{:T(128)} %constant.108.clone.1..sunk, s32[]{:T(128)} %constant.108.clone.1..sunk) | dynamic-update-slice | bytes 262148 | tf_op jit(solution)/shard_map/while/body/jit(dynamic_update_index_in_dim)/dynamic_update_slice | solution.py:159
  140.6 2.9 convolution_bitcast_fusion.7
  148.1 4.5 %dynamic_update_slice.17 = f32[8,128,16,16]{1,0,3,2:T(8,128)} dynamic-update-slice(f32[8,128,16,16]{1,0,3,2:T(8,128)} %get-tuple-element.763, f32[1,128,16,16]{1,0,3,2:T(1,128)S(1)} %bitcast.255, s32[]{:T(128)} %get-tuple-element.757, s32[]{:T(128)} %constant.108.clone.1..sunk, s32[]{:T(128)} %constant.108.clone.1..sunk, s32[]{:T(128)} %constant.108.clone.1..sunk) | dynamic-update-slice | bytes 262148 | tf_op jit(solution)/shard_map/while/body/jit(dynamic_update_index_in_dim)/dynamic_update_slice | solution.py:159
  157.7 2.9 convolution_bitcast_fusion.7
  165.1 4.5 %dynamic_update_slice.17 = f32[8,128,16,16]{1,0,3,2:T(8,128)} dynamic-update-slice(f32[8,128,16,16]{1,0,3,2:T(8,128)} %get-tuple-element.763, f32[1,128,16,16]{1,0,3,2:T(1,128)S(1)} %bitcast.255, s32[]{:T(128)} %get-tuple-element.757, s32[]{:T(128)} %constant.108.clone.1..sunk, s32[]{:T(128)} %constant.108.clone.1..sunk, s32[]{:T(128)} %constant.108.clone.1..sunk) | dynamic-update-slice | bytes 262148 | tf_op jit(solution)/shard_map/while/body/jit(dynamic_update_index_in_dim)/dynamic_update_slice | solution.py:159
  174.7 2.9 convolution_bitcast_fusion.7
  182.1 4.5 %dynamic_update_slice.17 = f32[8,128,16,16]{1,0,3,2:T(8,128)} dynamic-update-slice(f32[8,128,16,16]{1,0,3,2:T(8,128)} %get-tuple-element.763, f32[1,128,16,16]{1,0,3,2:T(1,128)S(1)} %bitcast.255, s32[]{:T(128)} %get-tuple-element.757, s32[]{:T(128)} %constant.108.clone.1..sunk, s32[]{:T(128)} %constant.108.clone.1..sunk, s32[]{:T(128)} %constant.108.clone.1..sunk) | dynamic-update-slice | bytes 262148 | tf_op jit(solution)/shard_map/while/body/jit(dynamic_update_index_in_dim)/dynamic_update_slice | solution.py:159
  188.6 5.8 %rev.28 = f32[16,128,128]{2,1,0:T(8,128)} reverse(f32[16,128,128]{2,1,0:T(8,128)S(1)} %get-tuple-element.253), dimensions={2} | reverse | bytes 2097152 | tf_op jit(solution)/shard_map/jit(_flip)/rev | solution.py:71
  198.6 6.2 %reshape.321 = f32[16,128,255]{2,1,0:T(8,128)} reshape(f32[16,32640]{1,0:T(8,128)} %slice.149) | data formatting | bytes 4177920 | tf_op jit(solution)/shard_map/reshape | solution.py:76
  209.7 5.0 %fusion.63 = f32[2,16,16,16]{1,3,0,2:T(8,128)} fusion(bf16[1024,16,16,1]{0,2,3,1:T(8,128)(2,1)} %bitcast.266, f32[1,16,16,1024]{3,2,0,1:T(8,128)} %negate_bitcast_fusion, f32[1,16,16,1024]{3,2,0,1:T(8,128)} %bitcast.263), kind=kOutput, calls=%fused_computation.91 | convolution fusion | flops 50855936 | bytes 2654208 | tf_op jit(solution)/shard_map/kgns,sgm->kngm/dot_general | solution.py:114
  219.7 2.9 fusion.70
  225.7 34.5 %shard_map.84 = f32[16,5,16,256]{3,2,1,0:T(8,128)} custom-call(f32[5,16,256]{2,1,0:T(8,128)} %pad_maximum_fusion.5.x_ref), custom_call_target="tpu_custom_call" | custom-call | tf_op jit(solution)/shard_map/pallas_call | solution.py:49
  262.9 3.1 multiply_reduce_fusion.2
  271.7 24.8 %shard_map.85 = f32[32,8,128]{2,1,0:T(8,128)} custom-call(f32[8,128]{1,0:T(8,128)} %broadcast_in_dim.101.x_ref), custom_call_target="tpu_custom_call" | custom-call | tf_op jit(solution)/shard_map/pallas_call | solution.py:49
  301.2 49.0 %while.40 = (s32[]{:T(128)}, f32[16,16,16]{0,2,1:T(8,128)S(1)}, f32[8,128,16,16]{1,0,3,2:T(8,128)}, f32[16,16,1]{0,1,2:T(8,128)S(1)}, f32[8,128,16,16]{1,3,2,0:T...) while((s32[]{:T(128)}, f32[16,16,16]{0,2,1:T(8,128)S(1)}, ...), condition=%wide.region_10.11_spmd.clone, body=%wide.region_9.10_spmd.clone.sunk | while | flops 62996484 | bytes 2277520 | solution.py:220
  302.4 4.5 %dynamic_update_slice.18 = f32[8,128,16,16]{1,0,3,2:T(8,128)} dynamic-update-slice(f32[8,128,16,16]{1,0,3,2:T(8,128)} %get-tuple-element.806, f32[1,128,16,16]{1,0,3,2:T(1,128)S(1)} %bitcast.256, s32[]{:T(128)S(6)} %sub.210, s32[]{:T(128)} %constant.108.clone.1..sunk.1, s32[]{:T(128)} %constant.108.clone.1..sunk.1, s32[]{:T(128)} %constant.108.clone.1..sunk.1) | dynamic-update-slice | bytes 262148 | tf_op jit(solution)/shard_map/while/body/jit(dynamic_update_index_in_dim)/dynamic_update_slice | solution.py:159
  308.5 4.5 %dynamic_update_slice.18 = f32[8,128,16,16]{1,0,3,2:T(8,128)} dynamic-update-slice(f32[8,128,16,16]{1,0,3,2:T(8,128)} %get-tuple-element.806, f32[1,128,16,16]{1,0,3,2:T(1,128)S(1)} %bitcast.256, s32[]{:T(128)S(6)} %sub.210, s32[]{:T(128)} %constant.108.clone.1..sunk.1, s32[]{:T(128)} %constant.108.clone.1..sunk.1, s32[]{:T(128)} %constant.108.clone.1..sunk.1) | dynamic-update-slice | bytes 262148 | tf_op jit(solution)/shard_map/while/body/jit(dynamic_update_index_in_dim)/dynamic_update_slice | solution.py:159
  314.7 4.5 %dynamic_update_slice.18 = f32[8,128,16,16]{1,0,3,2:T(8,128)} dynamic-update-slice(f32[8,128,16,16]{1,0,3,2:T(8,128)} %get-tuple-element.806, f32[1,128,16,16]{1,0,3,2:T(1,128)S(1)} %bitcast.256, s32[]{:T(128)S(6)} %sub.210, s32[]{:T(128)} %constant.108.clone.1..sunk.1, s32[]{:T(128)} %constant.108.clone.1..sunk.1, s32[]{:T(128)} %constant.108.clone.1..sunk.1) | dynamic-update-slice | bytes 262148 | tf_op jit(solution)/shard_map/while/body/jit(dynamic_update_index_in_dim)/dynamic_update_slice | solution.py:159
  320.8 4.5 %dynamic_update_slice.18 = f32[8,128,16,16]{1,0,3,2:T(8,128)} dynamic-update-slice(f32[8,128,16,16]{1,0,3,2:T(8,128)} %get-tuple-element.806, f32[1,128,16,16]{1,0,3,2:T(1,128)S(1)} %bitcast.256, s32[]{:T(128)S(6)} %sub.210, s32[]{:T(128)} %constant.108.clone.1..sunk.1, s32[]{:T(128)} %constant.108.clone.1..sunk.1, s32[]{:T(128)} %constant.108.clone.1..sunk.1) | dynamic-update-slice | bytes 262148 | tf_op jit(solution)/shard_map/while/body/jit(dynamic_update_index_in_dim)/dynamic_update_slice | solution.py:159
  326.9 4.5 %dynamic_update_slice.18 = f32[8,128,16,16]{1,0,3,2:T(8,128)} dynamic-update-slice(f32[8,128,16,16]{1,0,3,2:T(8,128)} %get-tuple-element.806, f32[1,128,16,16]{1,0,3,2:T(1,128)S(1)} %bitcast.256, s32[]{:T(128)S(6)} %sub.210, s32[]{:T(128)} %constant.108.clone.1..sunk.1, s32[]{:T(128)} %constant.108.clone.1..sunk.1, s32[]{:T(128)} %constant.108.clone.1..sunk.1) | dynamic-update-slice | bytes 262148 | tf_op jit(solution)/shard_map/while/body/jit(dynamic_update_index_in_dim)/dynamic_update_slice | solution.py:159
  333.0 4.5 %dynamic_update_slice.18 = f32[8,128,16,16]{1,0,3,2:T(8,128)} dynamic-update-slice(f32[8,128,16,16]{1,0,3,2:T(8,128)} %get-tuple-element.806, f32[1,128,16,16]{1,0,3,2:T(1,128)S(1)} %bitcast.256, s32[]{:T(128)S(6)} %sub.210, s32[]{:T(128)} %constant.108.clone.1..sunk.1, s32[]{:T(128)} %constant.108.clone.1..sunk.1, s32[]{:T(128)} %constant.108.clone.1..sunk.1) | dynamic-update-slice | bytes 262148 | tf_op jit(solution)/shard_map/while/body/jit(dynamic_update_index_in_dim)/dynamic_update_slice | solution.py:159
  339.2 4.5 %dynamic_update_slice.18 = f32[8,128,16,16]{1,0,3,2:T(8,128)} dynamic-update-slice(f32[8,128,16,16]{1,0,3,2:T(8,128)} %get-tuple-element.806, f32[1,128,16,16]{1,0,3,2:T(1,128)S(1)} %bitcast.256, s32[]{:T(128)S(6)} %sub.210, s32[]{:T(128)} %constant.108.clone.1..sunk.1, s32[]{:T(128)} %constant.108.clone.1..sunk.1, s32[]{:T(128)} %constant.108.clone.1..sunk.1) | dynamic-update-slice | bytes 262148 | tf_op jit(solution)/shard_map/while/body/jit(dynamic_update_index_in_dim)/dynamic_update_slice | solution.py:159
  345.3 4.5 %dynamic_update_slice.18 = f32[8,128,16,16]{1,0,3,2:T(8,128)} dynamic-update-slice(f32[8,128,16,16]{1,0,3,2:T(8,128)} %get-tuple-element.806, f32[1,128,16,16]{1,0,3,2:T(1,128)S(1)} %bitcast.256, s32[]{:T(128)S(6)} %sub.210, s32[]{:T(128)} %constant.108.clone.1..sunk.1, s32[]{:T(128)} %constant.108.clone.1..sunk.1, s32[]{:T(128)} %constant.108.clone.1..sunk.1) | dynamic-update-slice | bytes 262148 | tf_op jit(solution)/shard_map/while/body/jit(dynamic_update_index_in_dim)/dynamic_update_slice | solution.py:159
  350.2 2.5 reshape.324
  352.7 2.7 fusion.61
  357.1 2.4 reshape.317
  359.5 2.6 fusion.62
  362.1 2.0 fusion.66
  369.0 11.7 %collective-permute-done.1 = f32[3,2,256]{1,2,0:T(8,128)S(1)} collective-permute-done((f32[3,2,256]{1,2,0:T(8,128)S(1)}, f32[3,2,256]{1,2,0:T(8,128)S(1)}, u32[]{:S(2)}, u32[]{:S(2)}) %collective-permute-start.1) | collective-permute-done | bytes 6176 | tf_op jit(solution)/shard_map/ppermute | solution.py:66
  382.3 3.4 fusion.54
  385.6 2.6 copy.142
  (247 shorter events, 148.6 us)
Async XLA Ops:
  0.6 16.2 %copy-start.33 = (f32[3,3,256]{2,1,0:T(4,128)S(1)}, f32[3,3,256]{2,1,0:T(4,128)}, u32[]{:S(2)}) copy-start(f32[3,3,256]{2,1,0:T(4,128)} %param.12) | copy-start | bytes 27652
  0.6 16.7 %copy-start.32 = (f32[16,16]{1,0:T(8,128)S(1)}, f32[16,16]{1,0:T(8,128)}, u32[]{:S(2)}) copy-start(f32[16,16]{1,0:T(8,128)} %param.14) | copy-start | bytes 3076
  2.2 43.0 %collective-permute-start = (bf16[3,2,256]{1,2,0:T(8,128)(2,1)}, bf16[3,2,256]{1,2,0:T(8,128)(2,1)}, u32[]{:S(2)}, u32[]{:S(2)}) collective-permute-start(bf16[3,2,256]{1,2,0:T(8,128)(2,1)} %copy.114), channel_id=1, source_target_pairs={{0,1},{1,2},{2,3},{3,4},{4,5},{5,6},{6,7},{7,8},{8,9},{9,10},{10,1... | collective-permute-start | bytes 9224 | tf_op jit(solution)/shard_map/ppermute | solution.py:66
  9.4 9.8 %copy-start.18 = (f32[16,16]{0,1:T(8,128)}, f32[16,16]{0,1:T(8,128)S(1)}, u32[]{:S(2)}) copy-start(f32[16,16]{0,1:T(8,128)S(1)} %copy.117) | copy-start | bytes 3076
  17.5 8.6 %copy-start.19 = (f32[16,16]{0,1:T(8,128)}, f32[16,16]{0,1:T(8,128)S(1)}, u32[]{:S(2)}) copy-start(f32[16,16]{0,1:T(8,128)S(1)} %copy.118) | copy-start | bytes 3076
  20.9 6.1 %copy-start.15 = (f32[1,16,16,128]{3,2,0,1:T(8,128)S(1)}, f32[1,16,16,128]{3,2,0,1:T(8,128)}, u32[]{:S(2)}) copy-start(f32[1,16,16,128]{3,2,0,1:T(8,128)} %get-tuple-element.558) | copy-start | bytes 393220
  21.0 6.1 %copy-start.16 = (f32[1,16,16,128]{3,2,0,1:T(8,128)S(1)}, f32[1,16,16,128]{3,2,0,1:T(8,128)}, u32[]{:S(2)}) copy-start(f32[1,16,16,128]{3,2,0,1:T(8,128)} %get-tuple-element.559) | copy-start | bytes 393220
  21.0 6.8 %copy-start.30 = (f32[3,1,256]{2,1,0:T(1,128)S(1)}, f32[3,1,256]{2,1,0:T(1,128)}, u32[]{:S(2)}) copy-start(f32[3,1,256]{2,1,0:T(1,128)} %get-tuple-element.561) | copy-start | bytes 9220
  21.0 6.8 %copy-start.31 = (f32[3,1,256]{2,1,0:T(1,128)S(1)}, f32[3,1,256]{2,1,0:T(1,128)}, u32[]{:S(2)}) copy-start(f32[3,1,256]{2,1,0:T(1,128)} %get-tuple-element.562) | copy-start | bytes 9220
  21.0 7.4 %copy-start.21 = (pred[128,128]{1,0:T(8,128)(4,1)S(1)}, pred[128,128]{1,0:T(8,128)(4,1)}, u32[]{:S(2)}) copy-start(pred[128,128]{1,0:T(8,128)(4,1)} %fusion.88) | copy-start | bytes 49156
  26.1 3.0 copy-start.13
  27.1 5.8 %copy-start.14 = (bf16[1024,256]{1,0:T(8,128)(2,1)S(1)}, bf16[1024,256]{1,0:T(8,128)(2,1)}, u32[]{:S(2)}) copy-start(bf16[1024,256]{1,0:T(8,128)(2,1)} %param.15) | copy-start | bytes 1572868
  31.6 7.2 %copy-start.29 = (f32[16,16]{0,1:T(8,128)S(1)}, f32[16,16]{0,1:T(8,128)}, u32[]{:S(2)}) copy-start(f32[16,16]{0,1:T(8,128)} %get-tuple-element.569) | copy-start | bytes 3076
  33.1 18.4 %copy-start.11 = (bf16[1024,256]{0,1:T(8,128)(2,1)}, bf16[1024,256]{0,1:T(8,128)(2,1)S(1)}, u32[]{:S(2)}) copy-start(bf16[1024,256]{0,1:T(8,128)(2,1)S(1)} %copy.116) | copy-start | bytes 1572868
  33.1 12.2 %copy-start.23 = (f32[3,256]{1,0:T(4,128)S(1)}, f32[3,256]{1,0:T(4,128)}, u32[]{:S(2)}) copy-start(f32[3,256]{1,0:T(4,128)} %get-tuple-element.575) | copy-start | bytes 9220
  33.1 12.2 %copy-start.25 = (f32[3,256]{1,0:T(4,128)S(1)}, f32[3,256]{1,0:T(4,128)}, u32[]{:S(2)}) copy-start(f32[3,256]{1,0:T(4,128)} %get-tuple-element.576) | copy-start | bytes 9220
  33.1 12.2 %copy-start.27 = (f32[3,1,256]{2,0,1:T(4,128)S(1)}, f32[3,1,256]{2,0,1:T(4,128)}, u32[]{:S(2)}) copy-start(f32[3,1,256]{2,0,1:T(4,128)} %copy.188) | copy-start | bytes 9220
  39.1 11.0 %copy-start.17 = (f32[16,256]{1,0:T(8,128)}, f32[16,256]{1,0:T(8,128)S(1)}, u32[]{:S(2)}) copy-start(f32[16,256]{1,0:T(8,128)S(1)} %neg.43) | copy-start | bytes 49156
  50.1 1.8 copy-start
  51.9 1.4 copy-start.8
  204.8 13.3 %copy-start.9 = (f32[1024,256]{0,1:T(8,128)S(1)}, f32[1024,256]{0,1:T(8,128)}, u32[]{:S(2)}) copy-start(f32[1024,256]{0,1:T(8,128)} %copy-done.8) | copy-start | bytes 3145732
  260.2 5.8 %copy-start.10 = (f32[16,5,16,256]{3,2,1,0:T(8,128)S(1)}, f32[16,5,16,256]{3,2,1,0:T(8,128)}, u32[]{:S(2)}) copy-start(f32[16,5,16,256]{3,2,1,0:T(8,128)} %shard_map.84) | copy-start | bytes 3932164
  350.2 5.2 %copy-start.1 = (f32[3,1024,256]{1,2,0:T(8,128)S(1)}, f32[3,1024,256]{1,2,0:T(8,128)}, u32[]{:S(2)}) copy-start(f32[3,1024,256]{1,2,0:T(8,128)} %copy-done) | copy-start | bytes 9437188
  355.4 1.6 copy-start.20
  359.5 4.7 %copy-start.2 = (f32[1,1024,256]{1,2,0:T(8,128)S(1)}, f32[1,1024,256]{1,2,0:T(8,128)}, u32[]{:S(2)}) copy-start(f32[1,1024,256]{1,2,0:T(8,128)} %get-tuple-element.546) | copy-start | bytes 3145732
  359.5 4.7 %copy-start.4 = (f32[1,1024,256]{1,2,0:T(8,128)S(1)}, f32[1,1024,256]{1,2,0:T(8,128)}, u32[]{:S(2)}) copy-start(f32[1,1024,256]{1,2,0:T(8,128)} %get-tuple-element.547) | copy-start | bytes 3145732
  364.2 1.0 copy-start.6
  364.2 2.5 copy-start.22
  364.2 3.9 copy-start.12
  364.2 16.6 %copy-start.3 = (f32[1,1024,256]{1,2,0:T(8,128)S(1)}, f32[1,1024,256]{1,2,0:T(8,128)}, u32[]{:S(2)}) copy-start(f32[1,1024,256]{1,2,0:T(8,128)} %get-tuple-element.546) | copy-start | bytes 3145732
  364.2 16.6 %copy-start.5 = (f32[1,1024,256]{1,2,0:T(8,128)S(1)}, f32[1,1024,256]{1,2,0:T(8,128)}, u32[]{:S(2)}) copy-start(f32[1,1024,256]{1,2,0:T(8,128)} %get-tuple-element.547) | copy-start | bytes 3145732
  365.2 15.5 %collective-permute-start.1 = (f32[3,2,256]{1,2,0:T(8,128)S(1)}, f32[3,2,256]{1,2,0:T(8,128)S(1)}, u32[]{:S(2)}, u32[]{:S(2)}) collective-permute-start(f32[3,2,256]{1,2,0:T(8,128)S(1)} %slice.151), channel_id=1, source_target_pairs={{1,0},{2,1},{3,2},{4,3},{5,4},{6,5},{7,6},{8,7},{9,8},{10,9},{11,1... | collective-permute-start | bytes 18440 | tf_op jit(solution)/shard_map/ppermute | solution.py:66
  369.0 13.2 %copy-start.7 = (f32[1,1024,256]{1,2,0:T(8,128)S(1)}, f32[1,1024,256]{1,2,0:T(8,128)}, u32[]{:S(2)}) copy-start(f32[1,1024,256]{1,2,0:T(8,128)} %copy-done.6) | copy-start | bytes 3145732
  369.0 13.2 %copy-start.24 = (f32[3,256]{1,0:T(4,128)S(1)}, f32[3,256]{1,0:T(4,128)}, u32[]{:S(2)}) copy-start(f32[3,256]{1,0:T(4,128)} %get-tuple-element.575) | copy-start | bytes 9220
  369.0 13.2 %copy-start.26 = (f32[3,256]{1,0:T(4,128)S(1)}, f32[3,256]{1,0:T(4,128)}, u32[]{:S(2)}) copy-start(f32[3,256]{1,0:T(4,128)} %get-tuple-element.576) | copy-start | bytes 9220
  369.0 13.2 %copy-start.28 = (f32[3,1,256]{2,0,1:T(4,128)S(1)}, f32[3,1,256]{2,0,1:T(4,128)}, u32[]{:S(2)}) copy-start(f32[3,1,256]{2,0,1:T(4,128)} %copy.188) | copy-start | bytes 9220
